TPU v7x, 256 devices: a whole 4x4x8 slice. The times are simulated.
256 devices in a mesh: slide: 16 (over y, x), row: 4 (over z_hi, core), col: 4 (over z_lo).
Axes of the slice: x: 4, y: 4, z: 8 (z_hi: 2, z_lo: 4; z = z_hi * 4 + z_lo), core: 2. Of those that a mesh axis runs over, the one named last changes fastest.
Arguments:
- features: bfloat16 [16, 256, 512, 256], P('slide', 'row', 'col'), may hold values from -6 to 6
- out_grad: bfloat16 [16, 256, 512, 256], P('slide', 'row', 'col'), may hold values from -6 to 6
- depth_weight: bfloat16 [9, 256], replicated, may hold values from -2 to 2
- point_weight: bfloat16 [256, 256], P(('slide', 'row', 'col')), may hold values from -0.375 to 0.375
Outputs:
- feature_grad: bfloat16 [16, 256, 512, 256], P('slide', 'row', 'col')
- point_grad: float32 [256, 256], P(('slide', 'row', 'col'))
- depth_grad: float32 [9, 256], replicated
All inputs are finite; a program needn't handle non-finite values.
Results may differ from a plain program's by a relative error of at most 0.007.
Values may be sent and summed in bfloat16 or wider, within the bound.
No kernel may reach another device: no remote copies, remote signals or barrier semaphores. Data moves between devices by JAX's collectives and lax.ppermute only.
A program may use at most 128 MiB of HBM per device.

v0:
```python
import math
import jax
import jax.numpy as jnp
from jax import lax
from jax.sharding import PartitionSpec as P


def padded(block, sides, width):
    for axis, dim in sides:
        count = lax.axis_size(axis)
        forward = [(i, i + 1) for i in range(count - 1)]
        backward = [(target, source) for source, target in forward]
        low = lax.ppermute(
            lax.slice_in_dim(block, block.shape[dim] - width, None, axis=dim), axis, forward
        )
        high = lax.ppermute(lax.slice_in_dim(block, 0, width, axis=dim), axis, backward)
        block = jnp.concatenate([low, block, high], axis=dim)
    return block


def back_project(grad_flat, point_weight):
    return lax.dot_general(
        grad_flat,
        lax.all_gather(point_weight, ("slide", "row", "col"), axis=0, tiled=True),
        (((1,), (1,)), ((), ())),
        preferred_element_type=jnp.float32,
    ).astype(jnp.bfloat16)


def on_device(features, out_grad, depth_weight, point_weight):
    rows = features.shape[1]
    cols = features.shape[2]
    chans = features.shape[3]
    total = lax.axis_size("slide") * lax.axis_size("row") * lax.axis_size("col") * rows * cols
    scale = 1.0 / math.sqrt(total)
    grad_flat = out_grad[0].reshape(rows * cols, chans)
    feat_pad = padded(features, (("row", 1), ("col", 2)), 2)[0]
    mid_grad = back_project(grad_flat, point_weight).reshape(rows, cols, chans)
    grad_pad = padded(mid_grad[None], (("row", 1), ("col", 2)), 2)[0]
    taps = depth_weight.astype(jnp.float32)
    mid = jnp.zeros((rows, cols, chans), jnp.float32)
    back = jnp.zeros((rows, cols, chans), jnp.float32)
    mid_f = mid_grad.astype(jnp.float32)
    tap_terms = []
    for a in range(3):
        for b in range(3):
            window = feat_pad[2 * a : 2 * a + rows, 2 * b : 2 * b + cols].astype(jnp.float32)
            mid = mid + taps[a * 3 + b] * window
            back = back + taps[a * 3 + b] * grad_pad[
                4 - 2 * a : 4 - 2 * a + rows, 4 - 2 * b : 4 - 2 * b + cols
            ].astype(jnp.float32)
            tap_terms.append(jnp.sum(window * mid_f, axis=(0, 1)))
    mid_flat = mid.astype(jnp.bfloat16).reshape(rows * cols, chans)
    owned = lax.psum_scatter(
        lax.dot_general(
            mid_flat, grad_flat, (((0,), (0,)), ((), ())), preferred_element_type=jnp.float32
        ),
        ("slide", "row", "col"),
        scatter_dimension=0,
        tiled=True,
    )
    depth_grad = lax.psum(jnp.stack(tap_terms), ("slide", "row", "col")) * scale
    feature_grad = back.astype(jnp.bfloat16)[None]
    return (feature_grad, owned * scale, depth_grad)


def solution(mesh):
    placed = (
        P("slide", "row", "col", None),
        P("slide", "row", "col", None),
        P(),
        P(("slide", "row", "col"), None),
    )
    return jax.shard_map(
        on_device,
        mesh=mesh,
        in_specs=placed,
        out_specs=(P("slide", "row", "col", None), P(("slide", "row", "col"), None), P()),
        check_vma=False,
    )
```

profile of v0, /device:TPU:2, one launch (start us, length us, event | category | flops | bytes accessed | tf_op | source)
XLA Modules:
  0.0 971.7 jit_solution(7291026716896225350)
XLA Ops:
  7.2 0.0 all-reduce.3.cloned.1.call-start
  7.2 1.0 fusion.22
  8.2 0.0 copy-start.3
  8.2 1.7 collective-permute-start.4
  10.0 1.3 collective-permute-start.5
  11.3 2.5 constant_dynamic-update-slice_fusion.1
  13.8 6.4 collective-permute-done.5
  20.2 2.1 copy-done.1
  22.3 0.1 fusion.21
  22.4 2.9 collective-permute-start.6
  25.4 1.3 collective-permute-start.7
  26.7 585.9 %all-gather = bf16[256,1,256]{2,1,0:T(2,128)(2,1)S(1)} all-gather(bf16[1,1,256]{2,1,0:T(2,128)(2,1)S(1)} %bitcast.71), channel_id=1, replica_groups=mesh['slide'=16,'row'=4,'col'=4] {'slide','row','col'}, dimensions={0}, use_global_device_ids=true | all-gather | bytes 131584 | tf_op jit(solution)/shard_map/all_gather | solution.py:24
  612.6 0.0 collective-permute-done.6
  612.6 7.2 maximum_bitcast_fusion.1
  619.8 22.3 %fusion.17 = (f32[256]{0:T(256)S(1)}, f32[256]{0:T(256)S(1)}, f32[256]{0:T(256)S(1)}, f32[256]{0:T(256)S(1)}, f32[256]{0:T(256)S(1)}, /*index=5*/f32[256]{0:T(25...) fusion(bf16[68,132,256]{2,1,0:T(8,128)(2,1)} %maximum_bitcast_fusion.1, ...), kind=kOutput, calls=%fused_computation.36 | convolution fusion | flops 1134556928 | bytes 46277632 | tf_op jit(solution)/shard_map/dot_general | solution.py:22
  642.1 0.0 copy-start
  642.1 22.8 %fusion.8 = bf16[64,128,256]{2,1,0:T(8,128)(2,1)S(1)} fusion(f32[256]{0:T(256)S(1)} %bitcast.69, f32[256]{0:T(256)S(1)} %bitcast.67, f32[256]{0:T(256)S(1)} %bitcast.65, f32[256]{0:T(256)S(1)} %bitcast.63, f32[256]{0:T(256)S(1)} %bitcast.61, f32[256]{0:T(256)S(1)} %bitcast.59, f32[256]{0:T(256)S(1)} %bitcast.57, f32[256]{0:T(256)S(1)} %bitcast.55, ...), kind=kLoop, calls=%fused_computation.27 | loop fusion | flops 56623104 | bytes 41952256 | tf_op jit(solution)/shard_map/convert_element_type | solution.py:53
  665.0 2.0 fusion.25
  666.9 0.0 all-reduce.3.cloned.1.call-update
  667.0 111.4 %psum.7 = f32[9,256]{1,0:T(8,128)S(1)} all-reduce(f32[9,256]{1,0:T(8,128)S(1)} %stack.39), channel_id=1, replica_groups=mesh['slide'=16,'row'=4,'col'=4] {'slide','row','col'}, use_global_device_ids=true, to_apply=%region_10.0 | all-reduce | flops 2304 | bytes 18432 | tf_op jit(solution)/shard_map/psum | solution.py:62
  778.4 1.0 fusion.23
  779.4 1.7 collective-permute-start
  781.2 1.3 collective-permute-start.1
  782.5 0.6 broadcast_multiply_fusion
  783.1 2.5 collective-permute-done.1
  785.6 1.1 pad_maximum_fusion.2
  786.7 4.0 collective-permute-start.2
  790.7 1.3 collective-permute-start.3
  792.0 156.4 %all-reduce.3.cloned.1.call-done = f32[256,256]{1,0:T(8,128)} async-done(((f32[256,256]{1,0:T(8,128)}), f32[256,256]{1,0:T(8,128)}) %all-reduce.3.cloned.1.call-update) | async-done | bytes 262160
  948.4 1.3 dynamic-slice_multiply_fusion
  949.7 4.2 maximum_bitcast_fusion
  953.9 10.9 %fusion.18 = bf16[1,64,128,256]{3,2,1,0:T(8,128)(2,1)} fusion(bf16[68,132,256]{2,1,0:T(8,128)(2,1)S(1)} %maximum_bitcast_fusion, f32[256]{0:T(256)S(1)} %bitcast.70, f32[256]{0:T(256)S(1)} %bitcast.68, f32[256]{0:T(256)S(1)} %bitcast.66, f32[256]{0:T(256)S(1)} %bitcast.64, f32[256]{0:T(256)S(1)} %bitcast.62, f32[256]{0:T(256)S(1)} %bitcast.60, ...), kind=kLoop, calls=%fused_computation.40 | loop fusion | flops 56623104 | bytes 41952256 | tf_op jit(solution)/shard_map/broadcast_in_dim | solution.py:63
  (14 shorter events, 0.1 us)
Async XLA Ops:
  7.2 19.5 %copy-start.2 = (bf16[9,256]{1,0:T(8,128)(2,1)S(1)}, bf16[9,256]{1,0:T(8,128)(2,1)}, u32[]{:S(2)}) copy-start(bf16[9,256]{1,0:T(8,128)(2,1)} %param.6) | copy-start | bytes 13828
  7.2 941.2 %all-reduce.3.cloned.1.call-start = ((), (), s32[]{:S(2)}) async-start(), calls=%async_computation | async-start | bytes 524288
  8.2 18.5 %copy-start.3 = (bf16[1,256]{1,0:T(2,128)(2,1)S(1)}, bf16[1,256]{1,0:T(2,128)(2,1)}, u32[]{:S(2)}) copy-start(bf16[1,256]{1,0:T(2,128)(2,1)} %param.7) | copy-start | bytes 1540
  8.2 3.1 collective-permute-start.4
  10.0 10.2 %collective-permute-start.5 = (bf16[1,2,128,256]{3,2,1,0:T(8,128)(2,1)S(1)}, bf16[1,2,128,256]{3,2,1,0:T(8,128)(2,1)S(1)}, u32[]{:S(2)}, u32[]{:S(2)}) collective-permute-start(bf16[1,2,128,256]{3,2,1,0:T(8,128)(2,1)S(1)} %get-tuple-element.16), channel_id=1, source_target_pairs={{4,0},{8,4},{12,8},{5,1},{9,5},{13,9},{6,2},{10,6},{14,10},{7,3},{... | collective-permute-start | bytes 393224 | tf_op jit(solution)/shard_map/ppermute | solution.py:16
  20.2 2.1 copy-start.1
  22.4 590.2 %collective-permute-start.6 = (bf16[1,68,2,256]{3,2,1,0:T(2,128)(2,1)S(1)}, bf16[1,68,2,256]{3,2,1,0:T(2,128)(2,1)S(1)}, u32[]{:S(2)}, u32[]{:S(2)}) collective-permute-start(bf16[1,68,2,256]{3,2,1,0:T(2,128)(2,1)S(1)} %get-tuple-element.12), channel_id=1, source_target_pairs={{0,1},{1,2},{2,3},{4,5},{5,6},{6,7},{8,9},{9,10},{10,11},{12,13},{... | collective-permute-start | bytes 208904 | tf_op jit(solution)/shard_map/ppermute | solution.py:13
  25.4 587.2 %collective-permute-start.7 = (bf16[1,68,2,256]{3,2,1,0:T(2,128)(2,1)S(1)}, bf16[1,68,2,256]{3,2,1,0:T(2,128)(2,1)S(1)}, u32[]{:S(2)}, u32[]{:S(2)}) collective-permute-start(bf16[1,68,2,256]{3,2,1,0:T(2,128)(2,1)S(1)} %get-tuple-element.13), channel_id=1, source_target_pairs={{1,0},{2,1},{3,2},{5,4},{6,5},{7,6},{9,8},{10,9},{11,10},{13,12},{... | collective-permute-start | bytes 208904 | tf_op jit(solution)/shard_map/ppermute | solution.py:16
  642.1 22.8 %copy-start = (bf16[1,64,128,256]{3,2,1,0:T(8,128)(2,1)S(1)}, bf16[1,64,128,256]{3,2,1,0:T(8,128)(2,1)}, u32[]{:S(2)}) copy-start(bf16[1,64,128,256]{3,2,1,0:T(8,128)(2,1)} %param.5) | copy-start | bytes 12582916
  779.4 3.7 collective-permute-start
  781.2 4.4 collective-permute-start.1
  786.7 162.9 %collective-permute-start.2 = (bf16[1,68,2,256]{3,2,1,0:T(2,128)(2,1)S(1)}, bf16[1,68,2,256]{3,2,1,0:T(2,128)(2,1)S(1)}, u32[]{:S(2)}, u32[]{:S(2)}) collective-permute-start(bf16[1,68,2,256]{3,2,1,0:T(2,128)(2,1)S(1)} %get-tuple-element.14), channel_id=1, source_target_pairs={{0,1},{1,2},{2,3},{4,5},{5,6},{6,7},{8,9},{9,10},{10,11},{12,13},{... | collective-permute-start | bytes 208904 | tf_op jit(solution)/shard_map/ppermute | solution.py:13
  790.7 158.9 %collective-permute-start.3 = (bf16[1,68,2,256]{3,2,1,0:T(2,128)(2,1)S(1)}, bf16[1,68,2,256]{3,2,1,0:T(2,128)(2,1)S(1)}, u32[]{:S(2)}, u32[]{:S(2)}) collective-permute-start(bf16[1,68,2,256]{3,2,1,0:T(2,128)(2,1)S(1)} %get-tuple-element.15), channel_id=1, source_target_pairs={{1,0},{2,1},{3,2},{5,4},{6,5},{7,6},{9,8},{10,9},{11,10},{13,12},{... | collective-permute-start | bytes 208904 | tf_op jit(solution)/shard_map/ppermute | solution.py:16
Sparse Core Ops, SparseCore 0:
  667.1 281.2 all-reduce.2
where the time goes:
time: 972 us
  blocking collectives  697 us (72%)
  waiting for transfers between devices  165 us (17%)
  other arithmetic  48.2 us (5%)
  matrix products  24.3 us (2%)
  starting transfers between devices  15.6 us (2%)
  between operations  14.2 us (1%)
    all_gather x1, blocking collectives, back_project(): lax.all_gather(point_weight, ('slide', 'row', 'col'), axis=0, tiled=True)  586 us
    unnamed x2, waiting for transfers between devices  156 us
    psum x1, blocking collectives, on_device(): depth_grad = lax.psum(jnp.stack(tap_terms), ('slide', 'row', 'col')) * scale  111 us
    convert_element_type x1, other arithmetic, on_device(): mid_flat = mid.astype(jnp.bfloat16).reshape(rows * cols, chans)  22.8 us
    dot_general x1, matrix products, back_project(): lax.dot_general(grad_flat, lax.all_gather(point_weight, ('slide', 'row',...  22.3 us
  transfers between devices with their start and end apart: 9, of which 3 were waited for; matrix products, arithmetic and copies ran while one was open for 1% of the time, Pallas kernels for 0%

commit v1 on v0

--- a/solution.py
+++ b/solution.py
@@ -3,6 +3,12 @@
 import jax.numpy as jnp
 from jax import lax
 from jax.sharding import PartitionSpec as P
+
+
+def summed_here(x, axis):
+    parts = lax.all_gather(x, axis, axis=0, tiled=False)
+    result = parts.sum(axis=0)
+    return result
 
 
 def padded(block, sides, width):
@@ -59,7 +65,7 @@
         scatter_dimension=0,
         tiled=True,
     )
-    depth_grad = lax.psum(jnp.stack(tap_terms), ("slide", "row", "col")) * scale
+    depth_grad = summed_here(jnp.stack(tap_terms), ("slide", "row", "col")) * scale
     feature_grad = back.astype(jnp.bfloat16)[None]
     return (feature_grad, owned * scale, depth_grad)
 

time: 972 us -> 1630 us (1.68)
  waiting for transfers between devices: 165 us -> 946 us
  blocking collectives: 697 us -> 586 us
    all_gather x0 -> x1, waiting for transfers between devices: none -> 689 us  [summed_here(): parts = lax.all_gather(x, axis, axis=0, tiled=False)]
    psum x1 -> x0, blocking collectives: 111 us -> none  [on_device(): depth_grad = lax.psum(jnp.stack(tap_terms), ('slide', 'row', 'col')) * scale]
    unnamed x2 -> x3, waiting for transfers between devices: 156 us -> 248 us
  transfers between devices with their start and end apart: 9 -> 10, of which waited for: 3 -> 4; matrix products, arithmetic and copies ran while one was open for 1% -> 3% of each run, Pallas kernels for 0% -> 0%
where the time goes in v1:
time: 1630 us; the launch traced here: 1620 us
  waiting for transfers between devices  946 us (58%)
  blocking collectives  586 us (36%)
  other arithmetic  33.1 us (2%)
  matrix products  24.2 us (1%)
    all_gather x1, waiting for transfers between devices, summed_here(): parts = lax.all_gather(x, axis, axis=0, tiled=False)  689 us
    all_gather x1, blocking collectives, back_project(): lax.all_gather(point_weight, ('slide', 'row', 'col'), axis=0, tiled=True)  586 us
    unnamed x3, waiting for transfers between devices  248 us
  transfers between devices with their start and end apart: 10, of which 4 were waited for; matrix products, arithmetic and copies ran while one was open for 3% of the time, Pallas kernels for 0%

profile of v1, /device:TPU:2, one launch (start us, length us, event | category | flops | bytes accessed | tf_op | source)
XLA Modules:
  0.0 1621.9 jit_solution(12085309556738057197)
XLA Ops:
  7.2 0.0 all-reduce.3.cloned.1.call-start
  7.2 1.0 fusion.22
  8.2 1.7 collective-permute-start.4
  10.0 1.3 collective-permute-start.5
  11.3 2.5 constant_dynamic-update-slice_fusion.1
  13.8 6.4 collective-permute-done.5
  20.2 0.1 fusion.21
  20.3 2.9 collective-permute-start.6
  23.3 1.3 collective-permute-start.7
  24.6 585.9 %all-gather.1 = bf16[256,1,256]{2,1,0:T(2,128)(2,1)S(1)} all-gather(bf16[1,1,256]{2,1,0:T(2,128)(2,1)S(1)} %bitcast.73), channel_id=1, replica_groups=mesh['slide'=16,'row'=4,'col'=4] {'slide','row','col'}, dimensions={0}, use_global_device_ids=true | all-gather | bytes 131584 | tf_op jit(solution)/shard_map/all_gather | solution.py:30
  610.5 2.5 maximum_bitcast_fusion.1
  613.1 9.9 fusion.8
  623.0 2.0 fusion.25
  625.0 0.0 all-reduce.3.cloned.1.call-update
  625.1 0.2 all-gather.5.cloned.1.call-start
  625.3 22.2 %fusion.17 = (f32[256]{0:T(256)S(1)}, f32[256]{0:T(256)S(1)}, f32[256]{0:T(256)S(1)}, f32[256]{0:T(256)S(1)}, f32[256]{0:T(256)S(1)}, /*index=5*/f32[256]{0:T(25...) fusion(bf16[68,132,256]{2,1,0:T(8,128)(2,1)} %copy-done, ...), kind=kOutput, calls=%fused_computation.36 | convolution fusion | flops 1134556928 | bytes 46277632 | tf_op jit(solution)/shard_map/dot_general | solution.py:28
  647.4 1.2 stack.39
  648.7 0.0 all-gather.5.cloned.1.call-update
  648.7 1.0 fusion.23
  649.7 1.3 collective-permute-start
  651.0 1.3 collective-permute-start.1
  652.3 1.9 collective-permute-done.1
  654.2 1.1 pad_maximum_fusion.2
  655.4 1.3 collective-permute-start.2
  656.7 1.3 collective-permute-start.3
  658.0 248.1 %all-reduce.3.cloned.1.call-done = f32[256,256]{1,0:T(8,128)} async-done(((f32[256,256]{1,0:T(8,128)}), f32[256,256]{1,0:T(8,128)}) %all-reduce.3.cloned.1.call-update) | async-done | bytes 262160
  906.1 1.3 dynamic-slice_multiply_fusion
  907.4 4.2 maximum_bitcast_fusion
  911.6 10.9 fusion.18
  922.5 689.4 %all-gather.5.cloned.1.call-done = f32[256,9,256]{2,1,0:T(8,128)} async-done(((f32[1,9,256]{2,1,0:T(8,128)}), f32[256,9,256]{2,1,0:T(8,128)}) %all-gather.5.cloned.1.call-update) | async-done | bytes 2359312 | tf_op jit(solution)/shard_map/all_gather | solution.py:9
  1612.0 2.5 reduce_sum.99
  1614.5 0.6 broadcast_multiply_fusion
  (17 shorter events, 0.1 us)
Async XLA Ops:
  7.2 17.4 %copy-start.2 = (bf16[9,256]{1,0:T(8,128)(2,1)S(1)}, bf16[9,256]{1,0:T(8,128)(2,1)}, u32[]{:S(2)}) copy-start(bf16[9,256]{1,0:T(8,128)(2,1)} %param.6) | copy-start | bytes 13828
  7.2 898.9 %all-reduce.3.cloned.1.call-start = ((), (), s32[]{:S(2)}) async-start(), calls=%async_computation.1 | async-start | bytes 524288
  8.2 16.4 %copy-start.3 = (bf16[1,256]{1,0:T(2,128)(2,1)S(1)}, bf16[1,256]{1,0:T(2,128)(2,1)}, u32[]{:S(2)}) copy-start(bf16[1,256]{1,0:T(2,128)(2,1)} %param.7) | copy-start | bytes 1540
  8.2 3.1 collective-permute-start.4
  10.0 10.2 collective-permute-start.5
  20.3 590.2 %collective-permute-start.6 = (bf16[1,68,2,256]{3,2,1,0:T(2,128)(2,1)S(1)}, bf16[1,68,2,256]{3,2,1,0:T(2,128)(2,1)S(1)}, u32[]{:S(2)}, u32[]{:S(2)}) collective-permute-start(bf16[1,68,2,256]{3,2,1,0:T(2,128)(2,1)S(1)} %get-tuple-element.12), channel_id=1, source_target_pairs={{0,1},{1,2},{2,3},{4,5},{5,6},{6,7},{8,9},{9,10},{10,11},{12,13},{... | collective-permute-start | bytes 208904 | tf_op jit(solution)/shard_map/ppermute | solution.py:19
  23.3 587.2 %collective-permute-start.7 = (bf16[1,68,2,256]{3,2,1,0:T(2,128)(2,1)S(1)}, bf16[1,68,2,256]{3,2,1,0:T(2,128)(2,1)S(1)}, u32[]{:S(2)}, u32[]{:S(2)}) collective-permute-start(bf16[1,68,2,256]{3,2,1,0:T(2,128)(2,1)S(1)} %get-tuple-element.13), channel_id=1, source_target_pairs={{1,0},{2,1},{3,2},{5,4},{6,5},{7,6},{9,8},{10,9},{11,10},{13,12},{... | collective-permute-start | bytes 208904 | tf_op jit(solution)/shard_map/ppermute | solution.py:22
  613.0 10.0 copy-start
  613.1 10.0 copy-start.1
  625.1 986.9 %all-gather.5.cloned.1.call-start = ((), (), s32[]{:S(2)}) async-start(), calls=%async_computation | async-start | bytes 4210688 | tf_op jit(solution)/shard_map/all_gather | solution.py:9
  649.7 2.6 collective-permute-start
  651.0 3.2 collective-permute-start.1
  655.4 252.0 %collective-permute-start.2 = (bf16[1,68,2,256]{3,2,1,0:T(2,128)(2,1)S(1)}, bf16[1,68,2,256]{3,2,1,0:T(2,128)(2,1)S(1)}, u32[]{:S(2)}, u32[]{:S(2)}) collective-permute-start(bf16[1,68,2,256]{3,2,1,0:T(2,128)(2,1)S(1)} %get-tuple-element.14), channel_id=1, source_target_pairs={{0,1},{1,2},{2,3},{4,5},{5,6},{6,7},{8,9},{9,10},{10,11},{12,13},{... | collective-permute-start | bytes 208904 | tf_op jit(solution)/shard_map/ppermute | solution.py:19
  656.7 250.7 %collective-permute-start.3 = (bf16[1,68,2,256]{3,2,1,0:T(2,128)(2,1)S(1)}, bf16[1,68,2,256]{3,2,1,0:T(2,128)(2,1)S(1)}, u32[]{:S(2)}, u32[]{:S(2)}) collective-permute-start(bf16[1,68,2,256]{3,2,1,0:T(2,128)(2,1)S(1)} %get-tuple-element.15), channel_id=1, source_target_pairs={{1,0},{2,1},{3,2},{5,4},{6,5},{7,6},{9,8},{10,9},{11,10},{13,12},{... | collective-permute-start | bytes 208904 | tf_op jit(solution)/shard_map/ppermute | solution.py:22
Sparse Core Ops, SparseCore 0:
  625.2 280.8 all-reduce.2
  908.6 703.3 all-gather.4
